TPU v7x, 32 devices: a whole 2x2x4 slice. The times are simulated.
32 devices in a mesh: grp: 2 (over y), pos: 16 (over z, x, core).
Axes of the slice: x: 2, y: 2, z: 4, core: 2. Of those that a mesh axis runs over, the one named last changes fastest.
Arguments:
- object_field: float32 [2, 2048, 2048], P(None, 'grp', 'pos'), may hold values from -5 to 5
- probe_field: float32 [2, 256, 256], replicated, may hold values from -5 to 5
- patterns: float32 [96, 256, 256], P(('grp', 'pos')), may hold values from 0.05 to 5
- corners: int32 [2, 96], P(None, ('grp', 'pos')), may hold values from 0 to 1792, as said below
- counts: int32 [32], replicated, may hold values from 1 to 3, as said below
Outputs:
- object_new: float32 [2, 2048, 2048], P(None, 'grp', 'pos')
- probe_new: float32 [2, 256, 256], replicated
Inputs may be any that keep to these rules, and one draw needn't show every extreme that they name: `corners`: each slot's patch of 256 x 256 cells lies inside the object and inside its device's block of 1024 x 128 object cells extended by 128 cells on every side (the device at grp index a and pos index b holds rows a * 1024 to a * 1024 + 1023 and columns b * 128 to b * 128 + 127). The live slots of a device are its first counts[d] slots; some device has all 3 slots live.
All inputs are finite; a program needn't handle non-finite values.
Results may differ from a plain program's by a relative error of at most 0.00012.
Values sent between devices are 32-bit elements; how exact they have to be, the bound alone decides.
A program may use at most 64 MiB of HBM per device.

v0:
```python
import math

import jax
import jax.numpy as jnp
from jax import lax
from jax.sharding import PartitionSpec as P

M = 256
HALO = 128


step_object = 0.25
step_probe = 4.0


def padded(x, sides, width):
    for axis, dim in sides:
        peers, length = (lax.axis_size(axis), x.shape[dim])
        up = [(i, (i + 1) % peers) for i in range(peers - 1)]
        down = [(j, i) for i, j in up]
        last = lax.slice_in_dim(x, length - width, length, axis=dim)
        initial = lax.slice_in_dim(x, 0, width, axis=dim)
        before = lax.ppermute(last, axis, up)
        after = lax.ppermute(initial, axis, down)
        x = jnp.concatenate([before, x, after], axis=dim)
    return x


def product(left, right):
    return jnp.dot(left, right, precision=lax.Precision.HIGHEST, preferred_element_type=jnp.float32)


def left_mul(cos_part, sin_part, real_part, imag_part):
    return (
        product(cos_part, real_part) - product(sin_part, imag_part),
        product(cos_part, imag_part) + product(sin_part, real_part),
    )


def right_mul(real_part, imag_part, cos_part, sin_part):
    return (
        product(real_part, cos_part) - product(imag_part, sin_part),
        product(real_part, sin_part) + product(imag_part, cos_part),
    )


def dft_tables(order):
    indices = jnp.arange(order, dtype=jnp.int32)
    phases = indices[:, None] * indices[None, :] % order
    angles = phases.astype(jnp.float32) * (2.0 * math.pi / order)
    factor = 1.0 / math.sqrt(order)
    return (jnp.cos(angles) * factor, -jnp.sin(angles) * factor)


def far_field(wave, measured, cos_table, sin_table):
    front_re, front_im = left_mul(cos_table, sin_table, wave[0], wave[1])
    far_re, far_im = right_mul(front_re, front_im, cos_table, sin_table)
    excess = far_re * far_re + far_im * far_im - measured
    back_re, back_im = left_mul(cos_table, -sin_table, excess * far_re, excess * far_im)
    chi_re, chi_im = right_mul(back_re, back_im, cos_table, -sin_table)
    return jnp.stack((chi_re, chi_im))


def on_device(object_field, probe_field, patterns, corners, counts):
    tile_rows = object_field.shape[1]
    tile_cols = object_field.shape[2]
    slot_count = patterns.shape[0]
    pos_count = lax.axis_size("pos")
    grp_index = lax.axis_index("grp")
    pos_index = lax.axis_index("pos")
    device = grp_index * pos_count + pos_index
    own_count = counts[device]
    cos_table, sin_table = dft_tables(M)
    extended = padded(object_field, (("grp", 1), ("pos", 2)), HALO)
    row_local = corners[0] - grp_index * tile_rows + HALO
    col_local = corners[1] - pos_index * tile_cols + HALO

    def cut_patch(row_at, col_at):
        return lax.dynamic_slice(extended, (jnp.int32(0), row_at, col_at), (2, M, M))

    patches = jax.vmap(cut_patch)(row_local, col_local)
    waves = jnp.stack(
        (
            probe_field[0] * patches[:, 0] - probe_field[1] * patches[:, 1],
            probe_field[0] * patches[:, 1] + probe_field[1] * patches[:, 0],
        ),
        axis=1,
    )
    empty_results = jnp.zeros((slot_count, 2, M, M), jnp.float32)

    def solve_own(step, results):
        result = far_field(waves[step], patterns[step], cos_table, sin_table)
        return lax.dynamic_update_index_in_dim(results, result, step, 0)

    residuals = lax.fori_loop(0, own_count, solve_own, empty_results)

    def accumulate(step, totals):
        grad_ext, grad_probe = totals
        chi_re = residuals[step, 0]
        chi_im = residuals[step, 1]
        patch_re = patches[step, 0]
        patch_im = patches[step, 1]
        obj_part = jnp.stack(
            (
                probe_field[0] * chi_re + probe_field[1] * chi_im,
                probe_field[0] * chi_im - probe_field[1] * chi_re,
            )
        )
        prb_part = jnp.stack(
            (patch_re * chi_re + patch_im * chi_im, patch_re * chi_im - patch_im * chi_re)
        )
        anchor = (jnp.int32(0), row_local[step], col_local[step])
        current = lax.dynamic_slice(grad_ext, anchor, (2, M, M))
        grad_ext = lax.dynamic_update_slice(grad_ext, current + obj_part, anchor)
        return (grad_ext, grad_probe + prb_part)

    start_totals = (
        jnp.zeros(extended.shape, jnp.float32),
        jnp.zeros(probe_field.shape, jnp.float32),
    )
    grad_ext, grad_probe = lax.fori_loop(0, own_count, accumulate, start_totals)
    col_rims = jnp.concatenate((grad_ext[:, :, :HALO], grad_ext[:, :, -HALO:]), axis=2)
    col_arrived = padded(col_rims, (("pos", 2),), HALO)
    middle = grad_ext[:, :, HALO : HALO + tile_cols]
    middle = middle.at[:, :, :HALO].add(col_arrived[:, :, :HALO])
    middle = middle.at[:, :, tile_cols - HALO :].add(col_arrived[:, :, -HALO:])
    row_rims = jnp.concatenate((middle[:, :HALO], middle[:, -HALO:]), axis=1)
    row_arrived = padded(row_rims, (("grp", 1),), HALO)
    core = middle[:, HALO : HALO + tile_rows]
    core = core.at[:, :HALO].add(row_arrived[:, :HALO])
    core = core.at[:, tile_rows - HALO :].add(row_arrived[:, -HALO:])
    object_new = object_field - step_object * core
    live_total = jnp.sum(counts).astype(jnp.float32)
    share = lax.psum_scatter(grad_probe, "pos", scatter_dimension=1, tiled=True)
    share = lax.psum(share, "grp")
    row_share = M // pos_count
    mine = lax.dynamic_slice_in_dim(probe_field, pos_index * row_share, row_share, 1)
    new_rows = mine - step_probe * share / live_total
    probe_new = lax.all_gather(new_rows, "pos", axis=1, tiled=True)
    return (object_new, probe_new)


def solution(mesh):
    return jax.shard_map(
        on_device,
        mesh=mesh,
        in_specs=(
            P(None, "grp", "pos"),
            P(),
            P(("grp", "pos"), None, None),
            P(None, ("grp", "pos")),
            P(),
        ),
        out_specs=(P(None, "grp", "pos"), P()),
        check_vma=False,
    )
```

profile of v0, /device:TPU:0, one launch (start us, length us, event | category | flops | bytes accessed | tf_op | source)
XLA Modules:
  0.0 322.6 jit_solution(2919764576730867751)
XLA Ops:
  8.3 4.9 %collective-permute-start = (f32[2,128,128]{2,1,0:T(8,128)S(1)}, f32[2,128,128]{2,1,0:T(8,128)S(1)}, u32[]{:S(2)}, u32[]{:S(2)}) collective-permute-start(f32[2,128,128]{2,1,0:T(8,128)S(1)} %get-tuple-element.348), channel_id=1, source_target_pairs={{0,16},{1,17},{2,18},{3,19},{4,20},{5,21},{6,22},{7,23},{8,24},{9,... | collective-permute-start | bytes 393224 | tf_op jit(solution)/shard_map/ppermute | solution.py:23
  13.2 1.3 collective-permute-start.1
  14.5 1.4 collective-permute-done
  15.9 1.3 constant_dynamic-update-slice_fusion.1
  17.2 2.8 collective-permute-done.1
  20.1 1.4 collective-permute-start.2
  21.5 1.3 collective-permute-start.3
  24.4 3.7 %collective-permute-done.3 = f32[2,1280,128]{2,1,0:T(8,128)} collective-permute-done((f32[2,1280,128]{2,1,0:T(8,128)S(1)}, f32[2,1280,128]{2,1,0:T(8,128)}, u32[]{:S(2)}, u32[]{:S(2)}) %collective-permute-start.3) | collective-permute-done | bytes 1310752 | tf_op jit(solution)/shard_map/ppermute | solution.py:24
  28.2 3.4 %pad_maximum_fusion = f32[2,1280,384]{2,1,0:T(8,128)} fusion(f32[2,1280,128]{2,1,0:T(8,128)} %collective-permute-done.3, f32[2,1280,128]{2,1,0:T(8,128)S(1)} %constant_dynamic-update-slice_fusion, f32[2,1280,128]{2,1,0:T(8,128)S(1)} %collective-permute-done.2), kind=kLoop, calls=%fused_computation.139 | loop fusion | flops 1966080 | bytes 7864320 | tf_op jit(solution)/shard_map/concatenate | solution.py:25
  31.8 9.6 %while.33 = (s32[]{:T(128)}, f32[2,1280,384]{2,1,0:T(8,128)}, s32[3,3]{1,0:T(4,128)S(1)}, f32[3,2,256,256]{3,2,1,0:T(8,128)S(1)}, s32[]{:T(128)}) while((s32[]{:T(128)}, f32[2,1280,384]{2,1,0:T(8,128)}, s32[3,3]{1,0:T(4,128)S(1)}, f32[3,2,256,256]{3,2,1,0:T(8,128)S(1)}, s32[]{:T(128)}) %tuple.101), condition=%wide.while_cond.4, body=%wide.while_body.4.sunk | while | flops 2 | bytes 1048693 | solution.py:79
  32.4 2.5 bitcast_dynamic-update-slice_fusion.2
  35.7 2.5 bitcast_dynamic-update-slice_fusion.2
  38.9 2.5 bitcast_dynamic-update-slice_fusion.2
  41.6 1.3 pad_maximum_fusion.1
  42.9 1.3 broadcast_in_dim.20
  44.2 30.9 %while.34 = (s32[]{:T(128)}, f32[3,2,256,256]{3,2,1,0:T(8,128)}, s32[]{:T(128)}, f32[3,2,256,256]{3,2,1,0:T(8,128)}, f32[3,256,256]{2,1,0:T(8,128)}, /*index=5*/s32[]{:T(128)}, s32[]{:T(128)}, s32[]{:T(128)}, s32[]{}) while((s32[]{:T(128)}, f32[3,2,256,256]{3,2,1,0:T(8,128)}, s32[]{:T(128)}, ...), condition=%wide.region_1.2_spmd.clone.clone, body=%wide.region_0.1_spmd.clone.clone.sunk | while | flops 3238789120 | bytes 12320939 | solution.py:95
  44.9 2.4 fusion.179
  47.3 2.4 convolution_subtract_fusion.7
  49.8 1.5 fusion.180
  51.2 2.4 fusion.181
  53.7 2.4 convolution_add_fusion.6
  56.1 1.5 convolution_subtract_fusion.8
  57.6 1.5 fusion.182
  59.1 2.4 fusion.183
  61.5 1.5 fusion.186
  63.0 1.5 convolution_add_fusion.7
  64.5 1.5 fusion.184
  66.0 1.5 convolution_subtract_fusion.9
  67.5 1.5 fusion.188
  68.9 1.5 fusion.189
  70.4 1.5 fusion.185
  71.9 1.5 fusion.187
  75.1 2.1 broadcast_in_dim.18
  77.3 14.2 %while.32 = (s32[]{:T(128)}, f32[2,1280,384]{2,1,0:T(8,128)}, f32[2,256,256]{2,1,0:T(8,128)S(1)}, s32[]{:T(128)}, s32[3]{0:T(128)S(1)}, /*index=5*/s32[3]{0:T(12...) while((s32[]{:T(128)}, f32[2,1280,384]{2,1,0:T(8,128)}, ...), condition=%wide.region_3.4_spmd, body=%wide.region_2.3_spmd.sunk | while | flops 1310731 | bytes 6816019 | solution.py:121
  83.1 1.1 fusion.161
  84.2 1.4 maximum_add_fusion.3
  85.6 5.2 %dynamic_update_slice.13 = f32[2,1280,384]{2,1,0:T(8,128)} dynamic-update-slice(f32[2,1280,384]{2,1,0:T(8,128)} %get-tuple-element.545, f32[2,256,256]{2,1,0:T(8,128)S(1)} %get-tuple-element.473, s32[]{:T(128)} %constant.180.clone.1..sunk, s32[]{:T(128)S(6)} %select_n.163, s32[]{:T(128)S(6)} %select_n.164) | dynamic-update-slice | bytes 1048580 | tf_op jit(solution)/shard_map/while/body/dynamic_update_slice | solution.py:114
  91.5 3.2 fusion.116
  94.7 117.2 %collective-permute-start.4 = (f32[2,1280,128]{2,1,0:T(8,128)}, f32[2,1280,128]{2,1,0:T(8,128)S(1)}, u32[]{:S(2)}, u32[]{:S(2)}) collective-permute-start(f32[2,1280,128]{2,1,0:T(8,128)} %get-tuple-element.341), channel_id=1, source_target_pairs={{0,1},{1,2},{2,3},{3,4},{4,5},{5,6},{6,7},{7,8},{8,9},{9,10},{10,1... | collective-permute-start | bytes 3932168 | tf_op jit(solution)/shard_map/ppermute | solution.py:23
  212.0 1.3 collective-permute-start.5
  214.6 57.1 %reduce-scatter.2.cloned.1.call-done = f32[2,16,256]{2,1,0:T(8,128)} async-done(((f32[2,256,256]{2,1,0:T(8,128)}), f32[2,16,256]{2,1,0:T(8,128)}) %reduce-scatter.2.cloned.1.call-update) | async-done | bytes 32784 | tf_op jit(solution)/shard_map/reduce_scatter | solution.py:134
  271.7 9.0 %psum.7 = f32[2,16,256]{2,1,0:T(8,128)S(1)} all-reduce(f32[2,16,256]{2,1,0:T(8,128)} %reduce-scatter.2.cloned.1.call-done), channel_id=1, replica_groups=mesh['grp'=2,'pos'=16] {'grp'}, use_global_device_ids=true, to_apply=%region_5.6 | all-reduce | flops 8192 | bytes 65536 | tf_op jit(solution)/shard_map/psum | solution.py:135
  280.7 1.9 add_add_fusion
  282.7 2.4 collective-permute-start.6
  285.1 20.9 %all_gather.3 = f32[2,256,256]{2,1,0:T(8,128)S(1)} all-gather(f32[2,16,256]{2,1,0:T(8,128)S(1)} %divide_subtract_fusion), channel_id=1, replica_groups=mesh['grp'=2,'pos'=16] {'pos'}, dimensions={1}, use_global_device_ids=true | all-gather | bytes 557056 | tf_op jit(solution)/shard_map/all_gather | solution.py:139
  306.1 1.4 collective-permute-start.7
  307.5 6.3 %collective-permute-done.7 = f32[2,128,128]{2,1,0:T(8,128)S(1)} collective-permute-done((f32[2,128,128]{2,1,0:T(8,128)S(1)}, f32[2,128,128]{2,1,0:T(8,128)S(1)}, u32[]{:S(2)}, u32[]{:S(2)}) %collective-permute-start.7) | collective-permute-done | bytes 131104 | tf_op jit(solution)/shard_map/ppermute | solution.py:24
  313.9 1.1 multiply_subtract_fusion
  (49 shorter events, 8.7 us)
Async XLA Ops:
  7.2 15.6 %copy-start.5 = (s32[2,3]{1,0:T(2,128)S(1)}, s32[2,3]{1,0:T(2,128)}, u32[]{:S(2)}) copy-start(s32[2,3]{1,0:T(2,128)} %param.24) | copy-start | bytes 76
  7.2 15.7 %copy-start.6 = (s32[32]{0:T(128)S(1)}, s32[32]{0:T(128)}, u32[]{:S(2)}) copy-start(s32[32]{0:T(128)} %param.25) | copy-start | bytes 388
  7.2 16.4 %copy-start.1 = (f32[2,256,256]{2,1,0:T(8,128)S(1)}, f32[2,256,256]{2,1,0:T(8,128)}, u32[]{:S(2)}) copy-start(f32[2,256,256]{2,1,0:T(8,128)} %param.22) | copy-start | bytes 1572868
  7.2 264.5 %reduce-scatter.2.cloned.1.call-start = ((), (), s32[]{:S(2)}) async-start(), calls=%async_computation.1 | async-start | bytes 557056 | tf_op jit(solution)/shard_map/reduce_scatter | solution.py:134
  8.3 7.6 %collective-permute-start = (f32[2,128,128]{2,1,0:T(8,128)S(1)}, f32[2,128,128]{2,1,0:T(8,128)S(1)}, u32[]{:S(2)}, u32[]{:S(2)}) collective-permute-start(f32[2,128,128]{2,1,0:T(8,128)S(1)} %get-tuple-element.348), channel_id=1, source_target_pairs={{0,16},{1,17},{2,18},{3,19},{4,20},{5,21},{6,22},{7,23},{8,24},{9,... | collective-permute-start | bytes 393224 | tf_op jit(solution)/shard_map/ppermute | solution.py:23
  13.2 6.9 %collective-permute-start.1 = (f32[2,128,128]{2,1,0:T(8,128)S(1)}, f32[2,128,128]{2,1,0:T(8,128)S(1)}, u32[]{:S(2)}, u32[]{:S(2)}) collective-permute-start(f32[2,128,128]{2,1,0:T(8,128)S(1)} %get-tuple-element.347), channel_id=1, source_target_pairs={{16,0},{17,1},{18,2},{19,3},{20,4},{21,5},{22,6},{23,7},{24,8},{25... | collective-permute-start | bytes 393224 | tf_op jit(solution)/shard_map/ppermute | solution.py:24
  20.1 4.3 %collective-permute-start.2 = (f32[2,1280,128]{2,1,0:T(8,128)S(1)}, f32[2,1280,128]{2,1,0:T(8,128)S(1)}, u32[]{:S(2)}, u32[]{:S(2)}) collective-permute-start(f32[2,1280,128]{2,1,0:T(8,128)S(1)} %constant_dynamic-update-slice_fusion), channel_id=1, source_target_pairs={{0,1},{1,2},{2,3},{3,4},{4,5},{5,6},{6,7},{7,8},{8,9},{9,10},{10,1... | collective-permute-start | bytes 3932168 | tf_op jit(solution)/shard_map/ppermute | solution.py:23
  21.5 6.7 %collective-permute-start.3 = (f32[2,1280,128]{2,1,0:T(8,128)S(1)}, f32[2,1280,128]{2,1,0:T(8,128)}, u32[]{:S(2)}, u32[]{:S(2)}) collective-permute-start(f32[2,1280,128]{2,1,0:T(8,128)S(1)} %constant_dynamic-update-slice_fusion), channel_id=1, source_target_pairs={{1,0},{2,1},{3,2},{4,3},{5,4},{6,5},{7,6},{8,7},{9,8},{10,9},{11,1... | collective-permute-start | bytes 3932168 | tf_op jit(solution)/shard_map/ppermute | solution.py:24
  31.7 9.7 %copy-start.3 = (f32[256,256]{1,0:T(8,128)S(1)}, f32[256,256]{1,0:T(8,128)}, u32[]{:S(2)}) copy-start(f32[256,256]{1,0:T(8,128)} %get-tuple-element.349) | copy-start | bytes 786436
  31.7 9.7 %copy-start.4 = (f32[256,256]{1,0:T(8,128)S(1)}, f32[256,256]{1,0:T(8,128)}, u32[]{:S(2)}) copy-start(f32[256,256]{1,0:T(8,128)} %get-tuple-element.350) | copy-start | bytes 786436
  91.5 3.2 copy-start
  94.7 186.0 %collective-permute-start.4 = (f32[2,1280,128]{2,1,0:T(8,128)}, f32[2,1280,128]{2,1,0:T(8,128)S(1)}, u32[]{:S(2)}, u32[]{:S(2)}) collective-permute-start(f32[2,1280,128]{2,1,0:T(8,128)} %get-tuple-element.341), channel_id=1, source_target_pairs={{0,1},{1,2},{2,3},{3,4},{4,5},{5,6},{6,7},{7,8},{8,9},{9,10},{10,1... | collective-permute-start | bytes 3932168 | tf_op jit(solution)/shard_map/ppermute | solution.py:23
  212.0 68.8 %collective-permute-start.5 = (f32[2,1280,128]{2,1,0:T(8,128)S(1)}, f32[2,1280,128]{2,1,0:T(8,128)}, u32[]{:S(2)}, u32[]{:S(2)}) collective-permute-start(f32[2,1280,128]{2,1,0:T(8,128)S(1)} %get-tuple-element.342), channel_id=1, source_target_pairs={{1,0},{2,1},{3,2},{4,3},{5,4},{6,5},{7,6},{8,7},{9,8},{10,9},{11,1... | collective-permute-start | bytes 3932168 | tf_op jit(solution)/shard_map/ppermute | solution.py:24
  282.7 24.8 %collective-permute-start.6 = (f32[2,128,128]{2,1,0:T(8,128)S(1)}, f32[2,128,128]{2,1,0:T(8,128)S(1)}, u32[]{:S(2)}, u32[]{:S(2)}) collective-permute-start(f32[2,128,128]{2,1,0:T(8,128)S(1)} %get-tuple-element.346), channel_id=1, source_target_pairs={{0,16},{1,17},{2,18},{3,19},{4,20},{5,21},{6,22},{7,23},{8,24},{9,... | collective-permute-start | bytes 393224 | tf_op jit(solution)/shard_map/ppermute | solution.py:23
  306.0 7.9 %copy-start.2 = (f32[2,1024,128]{2,1,0:T(8,128)S(1)}, f32[2,1024,128]{2,1,0:T(8,128)}, u32[]{:S(2)}) copy-start(f32[2,1024,128]{2,1,0:T(8,128)} %param.21) | copy-start | bytes 3145732
  306.1 7.8 %collective-permute-start.7 = (f32[2,128,128]{2,1,0:T(8,128)S(1)}, f32[2,128,128]{2,1,0:T(8,128)S(1)}, u32[]{:S(2)}, u32[]{:S(2)}) collective-permute-start(f32[2,128,128]{2,1,0:T(8,128)S(1)} %get-tuple-element.345), channel_id=1, source_target_pairs={{16,0},{17,1},{18,2},{19,3},{20,4},{21,5},{22,6},{23,7},{24,8},{25... | collective-permute-start | bytes 393224 | tf_op jit(solution)/shard_map/ppermute | solution.py:24
Sparse Core Ops, SparseCore 0:
  213.4 58.2 reduce-scatter.1
where the time goes:
time: 325 us; the launch traced here: 323 us
  starting transfers between devices  131 us (40%)
  waiting for transfers between devices  71.5 us (22%)
  blocking collectives  29.9 us (9%)
  matrix products  28.4 us (9%)
  local copies, waits for them, and re-layouts  27.6 us (8%)
  between operations  15 us (5%)
  other arithmetic  11.9 us (4%)
  loops' own time  7.08 us (2%)
    ppermute x4, starting transfers between devices, padded(): before = lax.ppermute(last, axis, up)  126 us
    reduce_scatter x1, waiting for transfers between devices, on_device(): share = lax.psum_scatter(grad_probe, 'pos', scatter_dimension=1, tiled=True)  57.1 us
    dot_general x16, matrix products, product(): jnp.dot(left, right, precision=lax.Precision.HIGHEST, preferred_element_t...  28.4 us
    all_gather x1, blocking collectives, on_device(): probe_new = lax.all_gather(new_rows, 'pos', axis=1, tiled=True)  20.9 us
    ppermute x4, waiting for transfers between devices, padded(): after = lax.ppermute(initial, axis, down)  12.9 us
    gather x9, local copies, waits for them, and re-layouts  9.58 us
    psum x1, blocking collectives, on_device(): share = lax.psum(share, 'grp')  8.99 us
  transfers between devices with their start and end apart: 9, of which 5 were waited for; matrix products, arithmetic and copies ran while one was open for 1% of the time, Pallas kernels for 0%

commit v1 on v0

v1 whole, which is shorter than its diff:
```python
import functools

import jax
import jax.numpy as jnp
import numpy as np
from jax import lax
from jax.experimental import pallas as pl
from jax.experimental.pallas import tpu as pltpu
from jax.sharding import PartitionSpec as P

HALO = 128
STEP_OBJECT = 0.25
STEP_PROBE = 4.0
MESH = pl.DeviceIdType.MESH


def dft_tables(order):
    indices = np.arange(order, dtype=np.int64)
    angles = (indices[:, None] * indices[None, :] % order) * (2.0 * np.pi / order)
    cos = np.cos(angles) / np.sqrt(order)
    sin = -np.sin(angles) / np.sqrt(order)
    left = np.block([[cos, -sin], [sin, cos]])
    right = np.block([[cos, sin], [-sin, cos]])
    both = np.stack([left, right]).astype(np.float32)
    high = both.astype(jnp.bfloat16)
    low = (both - high.astype(np.float32)).astype(jnp.bfloat16)
    return np.stack([high, low], axis=1)


def split(x):
    high = x.astype(jnp.bfloat16)
    low = (x - high.astype(jnp.float32)).astype(jnp.bfloat16)
    return high, low


def dot(a, b):
    return jnp.dot(a, b, preferred_element_type=jnp.float32)


def table_left(tab, which, data):
    high, low = split(data)
    th, tl = tab[which, 0], tab[which, 1]
    return dot(th, high) + (dot(th, low) + dot(tl, high))


def table_right(data, tab, which):
    high, low = split(data)
    th, tl = tab[which, 0], tab[which, 1]
    return dot(high, th) + (dot(low, th) + dot(high, tl))


def kernel(sizes, corners, counts, obj_hbm, prb_hbm, pat_hbm, tab_hbm, obj_out, prb_out,
           ext, prb, pat, tab, nb, stage, corv, cor_recv, cor_smem,
           gmid, gsend, grecv, gacc, yrecv, gp, p1r, p1, p2r, p2, p3r, pnew,
           loc, yh, corsem, cors, patsem, gsem, ysem, csem, gysem, asem, agsem, gasem, casem):
    G, PN, S, TR, M = sizes
    grp, pos = lax.axis_index("grp"), lax.axis_index("pos")
    core, chip, chips = lax.rem(pos, 2), pos // 2, PN // 2
    half = M // 2
    h2 = half // G
    h3 = max(8, h2 // chips)
    owners = h2 // h3

    def at(g, p):
        return {"device_id": (g, p), "device_id_type": MESH}

    col_peer = [at(grp, lax.rem(pos + PN - 1, PN)), at(grp, lax.rem(pos + 1, PN))]
    row_peer = [at(lax.rem(grp + G - 1, G), pos), at(lax.rem(grp + 1, G), pos)]
    col_send, col_recv = [pos > 0, pos < PN - 1], [pos < PN - 1, pos > 0]
    row_send, row_recv = [grp > 0, grp < G - 1], [grp < G - 1, grp > 0]
    partner = at(grp, pos + 1 - 2 * core)

    def grp_at(k):
        return lax.rem(grp + k, G)

    def chip_at(k):
        return lax.rem(chip + k, chips)

    locals_ = [
        pltpu.make_async_copy(obj_hbm, ext.at[:, pl.ds(HALO, TR), :], loc.at[0]),
        pltpu.make_async_copy(prb_hbm, prb, loc.at[1]),
        pltpu.make_async_copy(pat_hbm, pat, loc.at[2]),
        pltpu.make_async_copy(tab_hbm, tab, loc.at[3]),
    ]
    for c in locals_:
        c.start()

    barrier = pltpu.get_barrier_semaphore()
    for d in range(2):
        @pl.when(col_send[d])
        def _():
            pl.semaphore_signal(barrier, inc=1, **col_peer[d])
    for k in range(1, G):
        pl.semaphore_signal(barrier, inc=1, **at(grp_at(k), pos))
    for k in range(1, chips):
        pl.semaphore_signal(barrier, inc=1, **at(grp, chip_at(k) * 2 + core))
    pl.semaphore_signal(barrier, inc=1, **partner)
    expected = (pos > 0).astype(jnp.int32) + (pos < PN - 1).astype(jnp.int32) + G + chips - 1

    lane = lax.broadcasted_iota(jnp.int32, (M, HALO), 1)
    row8 = lax.broadcasted_iota(jnp.int32, (8, 128), 0)
    packed = jnp.zeros((8, 128), jnp.int32)
    for s in range(S):
        packed = jnp.where(row8 == s, corners[0, s] - grp * TR + HALO, packed)
    corv[...] = packed
    zero = jnp.zeros((HALO, HALO), jnp.float32)
    for s in range(S):
        for c in range(2):
            for at_row in (0, HALO + M):
                gmid[s, c, pl.ds(at_row, HALO), :] = zero
                for d in range(2):
                    grecv[d, s, c, pl.ds(at_row, HALO), :] = zero
    gp[...] = jnp.zeros(gp.shape, jnp.float32)

    pl.semaphore_wait(barrier, expected)

    def cor_copy(d):
        return pltpu.make_async_remote_copy(corv, cor_recv.at[d], corsem.at[0, d], corsem.at[1, d], **col_peer[d])

    def halo_copy(d):
        src, dst = ((0, HALO + TR), (TR - HALO, 0))[d]
        return pltpu.make_async_remote_copy(
            obj_hbm.at[:, pl.ds(src, HALO), :], ext.at[:, pl.ds(dst, HALO), :], yh.at[0, d], yh.at[1, d], **row_peer[d])

    for d in range(2):
        @pl.when(col_send[d])
        def _():
            cor_copy(d).start()

        @pl.when(row_send[d])
        def _():
            halo_copy(d).start()
    for d in range(2):
        @pl.when(col_recv[d])
        def _():
            cor_copy(d).wait_recv()
            c = pltpu.make_async_copy(cor_recv.at[d], cor_smem.at[d], cors.at[d])
            c.start()
            c.wait()
    locals_[0].wait()
    for d in range(2):
        @pl.when(row_recv[d])
        def _():
            halo_copy(d).wait_recv()

    def patch_copy(d, s):
        return pltpu.make_async_remote_copy(
            stage.at[d, s], nb.at[d, s], patsem.at[0, d, s], patsem.at[1, d, s], **col_peer[d])

    def grad_copy(d, s):
        return pltpu.make_async_remote_copy(
            gsend.at[d, s], grecv.at[d, s, :, pl.ds(HALO, M), :], gsem.at[0, d, s], gsem.at[1, d, s], **col_peer[d])

    for s in range(S):
        for d in range(2):
            @pl.when(col_send[d])
            def _():
                r = jnp.clip(cor_smem[1 - d, s, 0], 0, TR + 2 * HALO - M)
                for c in range(2):
                    stage[d, s, c] = ext[c, pl.ds(r, M), :]
                patch_copy(d, s).start()

    for c in locals_[1:]:
        c.wait()
    own_count = counts[grp * PN + pos]

    def slot(s, carry):
        r = jnp.clip(corners[0, s] - grp * TR + HALO, 0, TR + 2 * HALO - M)
        shift = jnp.clip(corners[1, s] - pos * HALO + HALO, 0, HALO)
        for d in range(2):
            @pl.when(col_recv[d])
            def _():
                patch_copy(d, s).wait_recv()
        back = lax.rem(HALO - shift, HALO)
        forth = lax.rem(shift, HALO)
        first = lane < HALO - shift
        patch = []
        for c in range(2):
            mid = pltpu.roll(ext[c, pl.ds(r, M), :], back, 1)
            before = pltpu.roll(nb[1, s, c], back, 1)
            after = pltpu.roll(nb[0, s, c], back, 1)
            patch.append(jnp.concatenate([jnp.where(first, before, mid), jnp.where(first, mid, after)], axis=1))
        pr, pi = prb[0], prb[1]
        wave = jnp.concatenate([pr * patch[0] - pi * patch[1], pr * patch[1] + pi * patch[0]], axis=0)
        front = table_left(tab, 0, wave)
        far = table_right(jnp.concatenate([front[:M], front[M:]], axis=1), tab, 1)
        fr, fi = far[:, :M], far[:, M:]
        excess = fr * fr + fi * fi - pat[s]
        excess = jnp.where(jnp.full((M, M), s, jnp.int32) < own_count, excess, 0.0)
        back_ = table_left(tab, 1, jnp.concatenate([excess * fr, excess * fi], axis=0))
        chi = table_right(jnp.concatenate([back_[:M], back_[M:]], axis=1), tab, 0)
        cr, ci = chi[:, :M], chi[:, M:]
        parts = (pr * cr + pi * ci, pr * ci - pi * cr)
        gp[0] += patch[0] * cr + patch[1] * ci
        gp[1] += patch[0] * ci - patch[1] * cr
        tail = lane >= shift
        for c in range(2):
            g0 = pltpu.roll(parts[c][:, :HALO], forth, 1)
            g1 = pltpu.roll(parts[c][:, HALO:], forth, 1)
            gsend[0, s, c] = jnp.where(tail, g0, 0.0)
            gmid[s, c, pl.ds(HALO, M), :] = jnp.where(tail, g1, g0)
            gsend[1, s, c] = jnp.where(tail, 0.0, g1)
        for d in range(2):
            @pl.when(col_send[d])
            def _():
                grad_copy(d, s).start()
        return carry

    lax.fori_loop(0, S, slot, 0)

    core_copy = pltpu.make_async_remote_copy(
        gp.at[:, pl.ds((1 - core) * half, half), :], p1r, csem.at[0], csem.at[1], **partner)
    core_copy.start()
    core_copy.wait_recv()
    p1[...] = gp[:, pl.ds(pl.multiple_of(core * half, half), half), :] + p1r[...]

    def grp_copy(k):
        rows = pl.ds(pl.multiple_of(grp_at(k) * h2, h2), h2)
        return pltpu.make_async_remote_copy(
            p1.at[:, rows, :], p2r.at[k], gysem.at[0, k], gysem.at[1, k], **at(grp_at(k), pos))

    for k in range(1, G):
        grp_copy(k).start()

    for s in range(S):
        for d in range(2):
            @pl.when(col_recv[d])
            def _():
                grad_copy(d, s).wait_recv()

    def gather(chunk, carry):
        base = pl.multiple_of(chunk * HALO, HALO)
        totals = [jnp.zeros((HALO, HALO), jnp.float32)] * 2
        for s in range(S):
            off = jnp.clip(base - (corners[0, s] - grp * TR + HALO) + HALO, 0, HALO + M)
            totals = [totals[c] + gmid[s, c, pl.ds(off, HALO), :] for c in range(2)]
        for c in range(2):
            gacc[c, pl.ds(base, HALO), :] = totals[c]
        for d in range(2):
            @pl.when(col_recv[d])
            def _():
                for c in range(2):
                    total = gacc[c, pl.ds(base, HALO), :]
                    for s in range(S):
                        off = jnp.clip(base - cor_smem[d, s, 0] + HALO, 0, HALO + M)
                        total = total + grecv[d, s, c, pl.ds(off, HALO), :]
                    gacc[c, pl.ds(base, HALO), :] = total
        return carry

    lax.fori_loop(0, (TR + 2 * HALO) // HALO, gather, 0)

    def rim_copy(d):
        src = (0, HALO + TR)[d]
        return pltpu.make_async_remote_copy(
            gacc.at[:, pl.ds(src, HALO), :], yrecv.at[d], ysem.at[0, d], ysem.at[1, d], **row_peer[d])

    for d in range(2):
        @pl.when(row_send[d])
        def _():
            rim_copy(d).start()

    for k in range(1, G):
        grp_copy(k).wait_recv()
    total = p1[:, pl.ds(pl.multiple_of(grp * h2, h2), h2), :]
    for k in range(1, G):
        total = total + p2r[k]
    p2[...] = total

    def share_copy(k):
        q = lax.rem(chip_at(k), owners)
        rows = pl.ds(pl.multiple_of(q * h3, 8), h3)
        return pltpu.make_async_remote_copy(
            p2.at[:, rows, :], p3r.at[k], asem.at[0, k], asem.at[1, k], **at(grp, chip_at(k) * 2 + core))

    for k in range(1, chips):
        @pl.when(chip_at(k) < owners)
        def _():
            share_copy(k).start()

    obj_out[...] = ext[:, pl.ds(HALO, TR), :] - STEP_OBJECT * gacc[:, pl.ds(HALO, TR), :]
    for d in range(2):
        @pl.when(row_recv[d])
        def _():
            rim_copy(d).wait_recv()
            rows = pl.ds((TR - HALO, 0)[d], HALO)
            obj_out[:, rows, :] = obj_out[:, rows, :] - STEP_OBJECT * yrecv[d]

    live = counts[0]
    for i in range(1, G * PN):
        live = live + counts[i]

    def new_rows(owner):
        return pl.ds(pl.multiple_of(core * half + grp * h2 + lax.rem(owner, owners) * h3, 8), h3)

    @pl.when(chip < owners)
    def _():
        total = p2[:, pl.ds(pl.multiple_of(lax.rem(chip, owners) * h3, 8), h3), :]
        for k in range(1, chips):
            share_copy(k).wait_recv()
            total = total + p3r[k]
        divisor = jnp.full(total.shape, live, jnp.int32).astype(jnp.float32)
        pnew[:, new_rows(chip), :] = prb[:, new_rows(chip), :] - STEP_PROBE * total / divisor

    def spread_copy(k, owner):
        return pltpu.make_async_remote_copy(
            pnew.at[:, new_rows(owner), :], pnew.at[:, new_rows(owner), :], agsem.at[0, k], agsem.at[1, k],
            **at(grp, chip_at(k) * 2 + core))

    @pl.when(chip < owners)
    def _():
        for k in range(1, chips):
            spread_copy(k, chip).start()
    for k in range(1, chips):
        source = lax.rem(chip + chips - k, chips)

        @pl.when(source < owners)
        def _():
            spread_copy(k, source).wait_recv()

    def grp_spread(k, g):
        rows = pl.ds(pl.multiple_of(core * half + g * h2, h2), h2)
        return pltpu.make_async_remote_copy(
            pnew.at[:, rows, :], pnew.at[:, rows, :], gasem.at[0, k], gasem.at[1, k], **at(grp_at(k), pos))

    for k in range(1, G):
        grp_spread(k, grp).start()
    for k in range(1, G):
        grp_spread(k, lax.rem(grp + G - k, G)).wait_recv()

    def core_spread(c):
        rows = pl.ds(pl.multiple_of(c * half, half), half)
        return pltpu.make_async_remote_copy(pnew.at[:, rows, :], pnew.at[:, rows, :], casem.at[0], casem.at[1], **partner)

    core_spread(core).start()
    core_spread(1 - core).wait_recv()
    prb_out[...] = pnew[...]

    for d in range(2):
        @pl.when(col_send[d])
        def _():
            cor_copy(d).wait_send()
            for s in range(S):
                patch_copy(d, s).wait_send()
                grad_copy(d, s).wait_send()

        @pl.when(row_send[d])
        def _():
            halo_copy(d).wait_send()
            rim_copy(d).wait_send()
    core_copy.wait_send()
    for k in range(1, G):
        grp_copy(k).wait_send()
        grp_spread(k, grp).wait_send()
    for k in range(1, chips):
        @pl.when(chip_at(k) < owners)
        def _():
            share_copy(k).wait_send()

        @pl.when(chip < owners)
        def _():
            spread_copy(k, chip).wait_send()
    core_spread(core).wait_send()


def on_device(grp_size, pos_size, tables, object_field, probe_field, patterns, corners, counts):
    TR, S, M = object_field.shape[1], patterns.shape[0], probe_field.shape[1]
    chips, half = pos_size // 2, M // 2
    h2 = half // grp_size
    h3 = max(8, h2 // chips)
    f32 = jnp.float32
    V, D = pltpu.VMEM, pltpu.SemaphoreType.DMA
    smem = pl.BlockSpec(memory_space=pltpu.SMEM)
    hbm = pl.BlockSpec(memory_space=pl.ANY)
    vmem = pl.BlockSpec(memory_space=pltpu.VMEM)
    return pl.pallas_call(
        functools.partial(kernel, (grp_size, pos_size, S, TR, M)),
        out_shape=(
            jax.ShapeDtypeStruct(object_field.shape, f32),
            jax.ShapeDtypeStruct(probe_field.shape, f32),
        ),
        in_specs=[smem, smem, hbm, hbm, hbm, hbm],
        out_specs=(vmem, vmem),
        scratch_shapes=[
            V((2, TR + 2 * HALO, HALO), f32),
            V((2, M, M), f32),
            V((S, M, M), f32),
            V(tables.shape, jnp.bfloat16),
            V((2, S, 2, M, HALO), f32),
            V((2, S, 2, M, HALO), f32),
            V((8, 128), jnp.int32),
            V((2, 8, 128), jnp.int32),
            pltpu.SMEM((2, 8, 128), jnp.int32),
            V((S, 2, M + 2 * HALO, HALO), f32),
            V((2, S, 2, M, HALO), f32),
            V((2, S, 2, M + 2 * HALO, HALO), f32),
            V((2, TR + 2 * HALO, HALO), f32),
            V((2, 2, HALO, HALO), f32),
            V((2, M, M), f32),
            V((2, half, M), f32),
            V((2, half, M), f32),
            V((grp_size, 2, h2, M), f32),
            V((2, h2, M), f32),
            V((chips, 2, h3, M), f32),
            V((2, M, M), f32),
            D((4,)), D((2, 2)), D((2, 2)), D((2,)), D((2, 2, S)), D((2, 2, S)), D((2, 2)), D((2,)),
            D((2, grp_size)), D((2, chips)), D((2, chips)), D((2, grp_size)), D((2,)),
        ],
        compiler_params=pltpu.CompilerParams(
            collective_id=0, has_side_effects=True, vmem_limit_bytes=56 * 1024 * 1024
        ),
    )(corners, counts, object_field, probe_field, patterns, jnp.asarray(tables))


def solution(mesh):
    def body(object_field, probe_field, patterns, corners, counts):
        tables = dft_tables(probe_field.shape[1])
        return on_device(
            mesh.shape["grp"], mesh.shape["pos"], tables, object_field, probe_field, patterns, corners, counts
        )

    return jax.shard_map(
        body,
        mesh=mesh,
        in_specs=(
            P(None, "grp", "pos"),
            P(),
            P(("grp", "pos"), None, None),
            P(None, ("grp", "pos")),
            P(),
        ),
        out_specs=(P(None, "grp", "pos"), P()),
        check_vma=False,
    )
```

time: 325 us -> 68.9 us (0.21)
  starting transfers between devices: 131 us -> 0 us
  waiting for transfers between devices: 71.5 us -> 0 us
  Pallas kernels: 0 us -> 64.9 us
  blocking collectives: 29.9 us -> 0 us
  matrix products: 28.4 us -> 0 us
  local copies, waits for them, and re-layouts: 27.6 us -> 3.12 us
  between operations: 15 us -> 0.65 us
  other arithmetic: 11.9 us -> 0 us
  loops' own time: 7.08 us -> 0 us
    ppermute x8 -> x0, starting transfers between devices: 131 us -> none  [the longest x4 126 us: padded(): before = lax.ppermute(last, axis, up)]
    pallas_call x0 -> x1, Pallas kernels: none -> 64.9 us  [on_device(): pl.pallas_call(functools.partial(kernel, (grp_size, pos_size, S, TR, M)),...]
    reduce_scatter x1 -> x0, waiting for transfers between devices: 57.1 us -> none  [on_device(): share = lax.psum_scatter(grad_probe, 'pos', scatter_dimension=1, tiled=True)]
    dot_general x16 -> x0, matrix products: 28.4 us -> none  [product(): jnp.dot(left, right, precision=lax.Precision.HIGHEST, preferred_element_t...]
    all_gather x1 -> x0, blocking collectives: 20.9 us -> none  [on_device(): probe_new = lax.all_gather(new_rows, 'pos', axis=1, tiled=True)]
    ppermute x8 -> x0, waiting for transfers between devices: 14.3 us -> none  [the longest x4 12.9 us: padded(): after = lax.ppermute(initial, axis, down)]
    gather x9 -> x0, local copies, waits for them, and re-layouts: 9.58 us -> none
    psum x1 -> x0, blocking collectives: 8.99 us -> none  [on_device(): share = lax.psum(share, 'grp')]
  transfers between devices with their start and end apart: 9 -> 0, of which waited for: 5 -> 0; matrix products, arithmetic and copies ran while one was open for 1% -> 0% of each run, Pallas kernels for 0% -> 0%
where the time goes in v1:
time: 68.9 us; the launch traced here: 68.7 us
  Pallas kernels  64.9 us (94%)
  local copies, waits for them, and re-layouts  3.12 us (5%)
    pallas_call x1, Pallas kernels, on_device(): pl.pallas_call(functools.partial(kernel, (grp_size, pos_size, S, TR, M)),...  64.9 us
    unnamed x4, local copies, waits for them, and re-layouts  3.12 us

profile of v1, /device:TPU:0, one launch (start us, length us, event | category | flops | bytes accessed | tf_op | source)
XLA Modules:
  0.0 68.7 jit_solution(10868270564458982185)
XLA Ops:
  0.6 64.9 %shard_map.77 = (f32[2,1024,128]{2,1,0:T(8,128)}, f32[2,256,256]{2,1,0:T(8,128)}) custom-call(s32[2,3]{1,0:T(2,128)} %corners.1, s32[32]{0:T(128)} %counts.1, f32[2,1024,128]{2,1,0:T(8,128)} %obj_hbm.1, f32[2,256,256]{2,1,0:T(8,128)} %prb_hbm.1, f32[3,256,256]{2,1,0:T(8,128)} %pat_hbm.1, bf16[2,2,512,512]{3,2,1,0:T(8,128)(2,1)} %constant.2.clone.tab_hbm), custom_call_target="tpu_custom_call" | custom-call | tf_op jit(solution)/shard_map/pallas_call | solution.py:375
  65.5 0.0 copy-start
  65.6 2.3 %copy.10 = f32[2,1024,128]{2,1,0:T(8,128)} copy(f32[2,1024,128]{2,1,0:T(8,128)} %get-tuple-element.4) | data formatting | bytes 2097152
  67.9 0.0 copy-done
  67.9 0.8 %copy.11 = f32[2,256,256]{2,1,0:T(8,128)} copy(f32[2,256,256]{2,1,0:T(8,128)S(1)} %copy-done) | data formatting | bytes 1048576
Async XLA Ops:
  65.5 2.3 %copy-start = (f32[2,256,256]{2,1,0:T(8,128)S(1)}, f32[2,256,256]{2,1,0:T(8,128)}, u32[]{:S(2)}) copy-start(f32[2,256,256]{2,1,0:T(8,128)} %get-tuple-element.5) | copy-start | bytes 1572868

commit v2 on v1

--- a/solution.py
+++ b/solution.py
@@ -150,6 +150,11 @@
     def grad_copy(d, s):
         return pltpu.make_async_remote_copy(
             gsend.at[d, s], grecv.at[d, s, :, pl.ds(HALO, M), :], gsem.at[0, d, s], gsem.at[1, d, s], **col_peer[d])
+
+    def last_copy(d, c):
+        return pltpu.make_async_remote_copy(
+            gsend.at[d, S - 1, c], grecv.at[d, S - 1, c, pl.ds(HALO, M), :],
+            gsem.at[0, d, S - 1 + c], gsem.at[1, d, S - 1 + c], **col_peer[d])
 
     for s in range(S):
         for d in range(2):
@@ -201,7 +206,7 @@
             gmid[s, c, pl.ds(HALO, M), :] = jnp.where(tail, g1, g0)
             gsend[1, s, c] = jnp.where(tail, 0.0, g1)
         for d in range(2):
-            @pl.when(col_send[d])
+            @pl.when(col_send[d] & (s < S - 1))
             def _():
                 grad_copy(d, s).start()
         return carry
@@ -222,11 +227,81 @@
     for k in range(1, G):
         grp_copy(k).start()
 
-    for s in range(S):
-        for d in range(2):
-            @pl.when(col_recv[d])
-            def _():
+    for k in range(1, G):
+        grp_copy(k).wait_recv()
+    total = p1[:, pl.ds(pl.multiple_of(grp * h2, h2), h2), :]
+    for k in range(1, G):
+        total = total + p2r[k]
+    p2[...] = total
+
+    def share_copy(k):
+        q = lax.rem(chip_at(k), owners)
+        rows = pl.ds(pl.multiple_of(q * h3, 8), h3)
+        return pltpu.make_async_remote_copy(
+            p2.at[:, rows, :], p3r.at[k], asem.at[0, k], asem.at[1, k], **at(grp, chip_at(k) * 2 + core))
+
+    for k in range(1, chips):
+        @pl.when(chip_at(k) < owners)
+        def _():
+            share_copy(k).start()
+
+    for d in range(2):
+        @pl.when(col_send[d])
+        def _():
+            last_copy(d, 0).start()
+
+    live = counts[0]
+    for i in range(1, G * PN):
+        live = live + counts[i]
+
+    def new_rows(owner):
+        return pl.ds(pl.multiple_of(core * half + grp * h2 + lax.rem(owner, owners) * h3, 8), h3)
+
+    @pl.when(chip < owners)
+    def _():
+        total = p2[:, pl.ds(pl.multiple_of(lax.rem(chip, owners) * h3, 8), h3), :]
+        for k in range(1, chips):
+            share_copy(k).wait_recv()
+            total = total + p3r[k]
+        divisor = jnp.full(total.shape, live, jnp.int32).astype(jnp.float32)
+        pnew[:, new_rows(chip), :] = prb[:, new_rows(chip), :] - STEP_PROBE * total / divisor
+
+    def spread_copy(k, owner):
+        return pltpu.make_async_remote_copy(
+            pnew.at[:, new_rows(owner), :], pnew.at[:, new_rows(owner), :], agsem.at[0, k], agsem.at[1, k],
+            **at(grp, chip_at(k) * 2 + core))
+
+    @pl.when(chip < owners)
+    def _():
+        for k in range(1, chips):
+            spread_copy(k, chip).start()
+    for d in range(2):
+        @pl.when(col_send[d])
+        def _():
+            last_copy(d, 1).start()
+
+    for k in range(1, chips):
+        source = lax.rem(chip + chips - k, chips)
+
+        @pl.when(source < owners)
+        def _():
+            spread_copy(k, source).wait_recv()
+
+    def grp_spread(k, g):
+        rows = pl.ds(pl.multiple_of(core * half + g * h2, h2), h2)
+        return pltpu.make_async_remote_copy(
+            pnew.at[:, rows, :], pnew.at[:, rows, :], gasem.at[0, k], gasem.at[1, k], **at(grp_at(k), pos))
+
+    for k in range(1, G):
+        grp_spread(k, grp).start()
+
+    for d in range(2):
+        @pl.when(col_recv[d])
+        def _():
+            for s in range(S - 1):
                 grad_copy(d, s).wait_recv()
+            for c in range(2):
+                last_copy(d, c).wait_recv()
 
     def gather(chunk, carry):
         base = pl.multiple_of(chunk * HALO, HALO)
@@ -260,22 +335,13 @@
             rim_copy(d).start()
 
     for k in range(1, G):
-        grp_copy(k).wait_recv()
-    total = p1[:, pl.ds(pl.multiple_of(grp * h2, h2), h2), :]
-    for k in range(1, G):
-        total = total + p2r[k]
-    p2[...] = total
-
-    def share_copy(k):
-        q = lax.rem(chip_at(k), owners)
-        rows = pl.ds(pl.multiple_of(q * h3, 8), h3)
-        return pltpu.make_async_remote_copy(
-            p2.at[:, rows, :], p3r.at[k], asem.at[0, k], asem.at[1, k], **at(grp, chip_at(k) * 2 + core))
-
-    for k in range(1, chips):
-        @pl.when(chip_at(k) < owners)
-        def _():
-            share_copy(k).start()
+        grp_spread(k, lax.rem(grp + G - k, G)).wait_recv()
+
+    def core_spread(c):
+        rows = pl.ds(pl.multiple_of(c * half, half), half)
+        return pltpu.make_async_remote_copy(pnew.at[:, rows, :], pnew.at[:, rows, :], casem.at[0], casem.at[1], **partner)
+
+    core_spread(core).start()
 
     obj_out[...] = ext[:, pl.ds(HALO, TR), :] - STEP_OBJECT * gacc[:, pl.ds(HALO, TR), :]
     for d in range(2):
@@ -285,53 +351,6 @@
             rows = pl.ds((TR - HALO, 0)[d], HALO)
             obj_out[:, rows, :] = obj_out[:, rows, :] - STEP_OBJECT * yrecv[d]
 
-    live = counts[0]
-    for i in range(1, G * PN):
-        live = live + counts[i]
-
-    def new_rows(owner):
-        return pl.ds(pl.multiple_of(core * half + grp * h2 + lax.rem(owner, owners) * h3, 8), h3)
-
-    @pl.when(chip < owners)
-    def _():
-        total = p2[:, pl.ds(pl.multiple_of(lax.rem(chip, owners) * h3, 8), h3), :]
-        for k in range(1, chips):
-            share_copy(k).wait_recv()
-            total = total + p3r[k]
-        divisor = jnp.full(total.shape, live, jnp.int32).astype(jnp.float32)
-        pnew[:, new_rows(chip), :] = prb[:, new_rows(chip), :] - STEP_PROBE * total / divisor
-
-    def spread_copy(k, owner):
-        return pltpu.make_async_remote_copy(
-            pnew.at[:, new_rows(owner), :], pnew.at[:, new_rows(owner), :], agsem.at[0, k], agsem.at[1, k],
-            **at(grp, chip_at(k) * 2 + core))
-
-    @pl.when(chip < owners)
-    def _():
-        for k in range(1, chips):
-            spread_copy(k, chip).start()
-    for k in range(1, chips):
-        source = lax.rem(chip + chips - k, chips)
-
-        @pl.when(source < owners)
-        def _():
-            spread_copy(k, source).wait_recv()
-
-    def grp_spread(k, g):
-        rows = pl.ds(pl.multiple_of(core * half + g * h2, h2), h2)
-        return pltpu.make_async_remote_copy(
-            pnew.at[:, rows, :], pnew.at[:, rows, :], gasem.at[0, k], gasem.at[1, k], **at(grp_at(k), pos))
-
-    for k in range(1, G):
-        grp_spread(k, grp).start()
-    for k in range(1, G):
-        grp_spread(k, lax.rem(grp + G - k, G)).wait_recv()
-
-    def core_spread(c):
-        rows = pl.ds(pl.multiple_of(c * half, half), half)
-        return pltpu.make_async_remote_copy(pnew.at[:, rows, :], pnew.at[:, rows, :], casem.at[0], casem.at[1], **partner)
-
-    core_spread(core).start()
     core_spread(1 - core).wait_recv()
     prb_out[...] = pnew[...]
 
@@ -339,9 +358,12 @@
         @pl.when(col_send[d])
         def _():
             cor_copy(d).wait_send()
+            for c in range(2):
+                last_copy(d, c).wait_send()
             for s in range(S):
                 patch_copy(d, s).wait_send()
-                grad_copy(d, s).wait_send()
+                if s < S - 1:
+                    grad_copy(d, s).wait_send()
 
         @pl.when(row_send[d])
         def _():
@@ -375,8 +397,8 @@
     return pl.pallas_call(
         functools.partial(kernel, (grp_size, pos_size, S, TR, M)),
         out_shape=(
-            jax.ShapeDtypeStruct(object_field.shape, f32),
-            jax.ShapeDtypeStruct(probe_field.shape, f32),
+            pltpu.VMEM(object_field.shape, f32),
+            pltpu.VMEM(probe_field.shape, f32),
         ),
         in_specs=[smem, smem, hbm, hbm, hbm, hbm],
         out_specs=(vmem, vmem),
@@ -402,7 +424,7 @@
             V((2, h2, M), f32),
             V((chips, 2, h3, M), f32),
             V((2, M, M), f32),
-            D((4,)), D((2, 2)), D((2, 2)), D((2,)), D((2, 2, S)), D((2, 2, S)), D((2, 2)), D((2,)),
+            D((4,)), D((2, 2)), D((2, 2)), D((2,)), D((2, 2, S)), D((2, 2, S + 1)), D((2, 2)), D((2,)),
             D((2, grp_size)), D((2, chips)), D((2, chips)), D((2, grp_size)), D((2,)),
         ],
         compiler_params=pltpu.CompilerParams(

time: 68.9 us -> 64.9 us (0.942)
  Pallas kernels: 64.9 us -> 62.3 us
  local copies, waits for them, and re-layouts: 3.12 us -> 1.77 us
    pallas_call x1, Pallas kernels: 64.9 us -> 62.3 us  [on_device(): pl.pallas_call(functools.partial(kernel, (grp_size, pos_size, S, TR, M)),...]
    unnamed x4 -> x2, local copies, waits for them, and re-layouts: 3.12 us -> 1.77 us
where the time goes in v2:
time: 64.9 us; the launch traced here: 64.7 us
  Pallas kernels  62.3 us (96%)
  local copies, waits for them, and re-layouts  1.77 us (3%)
    pallas_call x1, Pallas kernels, on_device(): pl.pallas_call(functools.partial(kernel, (grp_size, pos_size, S, TR, M)),...  62.3 us
    unnamed x2, local copies, waits for them, and re-layouts  1.77 us

profile of v2, /device:TPU:0, one launch (start us, length us, event | category | flops | bytes accessed | tf_op | source)
XLA Modules:
  0.0 64.7 jit_solution(7200222715688595140)
XLA Ops:
  0.6 62.3 %shard_map.77 = (f32[2,1024,128]{2,1,0:T(8,128)S(1)}, f32[2,256,256]{2,1,0:T(8,128)S(1)}) custom-call(s32[2,3]{1,0:T(2,128)} %corners.1, s32[32]{0:T(128)} %counts.1, f32[2,1024,128]{2,1,0:T(8,128)} %obj_hbm.1, f32[2,256,256]{2,1,0:T(8,128)} %prb_hbm.1, f32[3,256,256]{2,1,0:T(8,128)} %pat_hbm.1, bf16[2,2,512,512]{3,2,1,0:T(8,128)(2,1)} %constant.2.clone.tab_hbm), custom_call_target="tpu_custom_call" | custom-call | tf_op jit(solution)/shard_map/pallas_call | solution.py:397
  63.0 1.0 %copy.10 = f32[2,1024,128]{2,1,0:T(8,128)} copy(f32[2,1024,128]{2,1,0:T(8,128)S(1)} %get-tuple-element.2) | data formatting | bytes 2097152
  63.9 0.8 %copy.11 = f32[2,256,256]{2,1,0:T(8,128)} copy(f32[2,256,256]{2,1,0:T(8,128)S(1)} %get-tuple-element.3) | data formatting | bytes 1048576

commit v3 on v2

--- a/solution.py
+++ b/solution.py
@@ -147,14 +147,10 @@
         return pltpu.make_async_remote_copy(
             stage.at[d, s], nb.at[d, s], patsem.at[0, d, s], patsem.at[1, d, s], **col_peer[d])
 
-    def grad_copy(d, s):
-        return pltpu.make_async_remote_copy(
-            gsend.at[d, s], grecv.at[d, s, :, pl.ds(HALO, M), :], gsem.at[0, d, s], gsem.at[1, d, s], **col_peer[d])
-
-    def last_copy(d, c):
-        return pltpu.make_async_remote_copy(
-            gsend.at[d, S - 1, c], grecv.at[d, S - 1, c, pl.ds(HALO, M), :],
-            gsem.at[0, d, S - 1 + c], gsem.at[1, d, S - 1 + c], **col_peer[d])
+    def grad_copy(d, s, c):
+        return pltpu.make_async_remote_copy(
+            gsend.at[d, s, c], grecv.at[d, s, c, pl.ds(HALO, M), :],
+            gsem.at[0, d, s, c], gsem.at[1, d, s, c], **col_peer[d])
 
     for s in range(S):
         for d in range(2):
@@ -208,7 +204,11 @@
         for d in range(2):
             @pl.when(col_send[d] & (s < S - 1))
             def _():
-                grad_copy(d, s).start()
+                grad_copy(d, s, 0).start()
+
+            @pl.when(col_send[d] & (s < S - 2))
+            def _():
+                grad_copy(d, s, 1).start()
         return carry
 
     lax.fori_loop(0, S, slot, 0)
@@ -248,7 +248,8 @@
     for d in range(2):
         @pl.when(col_send[d])
         def _():
-            last_copy(d, 0).start()
+            if S > 1:
+                grad_copy(d, S - 2, 1).start()
 
     live = counts[0]
     for i in range(1, G * PN):
@@ -278,7 +279,8 @@
     for d in range(2):
         @pl.when(col_send[d])
         def _():
-            last_copy(d, 1).start()
+            for c in range(2):
+                grad_copy(d, S - 1, c).start()
 
     for k in range(1, chips):
         source = lax.rem(chip + chips - k, chips)
@@ -298,13 +300,11 @@
     for d in range(2):
         @pl.when(col_recv[d])
         def _():
-            for s in range(S - 1):
-                grad_copy(d, s).wait_recv()
-            for c in range(2):
-                last_copy(d, c).wait_recv()
-
-    def gather(chunk, carry):
-        base = pl.multiple_of(chunk * HALO, HALO)
+            for s in range(S):
+                for c in range(2):
+                    grad_copy(d, s, c).wait_recv()
+
+    def gather(base):
         totals = [jnp.zeros((HALO, HALO), jnp.float32)] * 2
         for s in range(S):
             off = jnp.clip(base - (corners[0, s] - grp * TR + HALO) + HALO, 0, HALO + M)
@@ -320,9 +320,20 @@
                         off = jnp.clip(base - cor_smem[d, s, 0] + HALO, 0, HALO + M)
                         total = total + grecv[d, s, c, pl.ds(off, HALO), :]
                     gacc[c, pl.ds(base, HALO), :] = total
+
+    def gather_rim(chunk, carry):
+        gather(pl.multiple_of(chunk * (TR + HALO), HALO))
         return carry
 
-    lax.fori_loop(0, (TR + 2 * HALO) // HALO, gather, 0)
+    def gather_core(chunk, carry):
+        base = pl.multiple_of(chunk * HALO + HALO, HALO)
+        gather(base)
+        for c in range(2):
+            obj_out[c, pl.ds(pl.multiple_of(chunk * HALO, HALO), HALO), :] = (
+                ext[c, pl.ds(base, HALO), :] - STEP_OBJECT * gacc[c, pl.ds(base, HALO), :])
+        return carry
+
+    lax.fori_loop(0, 2, gather_rim, 0)
 
     def rim_copy(d):
         src = (0, HALO + TR)[d]
@@ -343,7 +354,7 @@
 
     core_spread(core).start()
 
-    obj_out[...] = ext[:, pl.ds(HALO, TR), :] - STEP_OBJECT * gacc[:, pl.ds(HALO, TR), :]
+    lax.fori_loop(0, TR // HALO, gather_core, 0)
     for d in range(2):
         @pl.when(row_recv[d])
         def _():
@@ -358,12 +369,10 @@
         @pl.when(col_send[d])
         def _():
             cor_copy(d).wait_send()
-            for c in range(2):
-                last_copy(d, c).wait_send()
             for s in range(S):
                 patch_copy(d, s).wait_send()
-                if s < S - 1:
-                    grad_copy(d, s).wait_send()
+                for c in range(2):
+                    grad_copy(d, s, c).wait_send()
 
         @pl.when(row_send[d])
         def _():
@@ -424,7 +433,7 @@
             V((2, h2, M), f32),
             V((chips, 2, h3, M), f32),
             V((2, M, M), f32),
-            D((4,)), D((2, 2)), D((2, 2)), D((2,)), D((2, 2, S)), D((2, 2, S + 1)), D((2, 2)), D((2,)),
+            D((4,)), D((2, 2)), D((2, 2)), D((2,)), D((2, 2, S)), D((2, 2, S, 2)), D((2, 2)), D((2,)),
             D((2, grp_size)), D((2, chips)), D((2, chips)), D((2, grp_size)), D((2,)),
         ],
         compiler_params=pltpu.CompilerParams(

time: 64.9 us -> 63.6 us (0.980)
  Pallas kernels: 62.3 us -> 61 us
    pallas_call x1, Pallas kernels: 62.3 us -> 61 us  [on_device(): pl.pallas_call(functools.partial(kernel, (grp_size, pos_size, S, TR, M)),...]
where the time goes in v3:
time: 63.6 us; the launch traced here: 63.4 us
  Pallas kernels  61 us (96%)
  local copies, waits for them, and re-layouts  1.77 us (3%)
  between operations  0.64 us (1%)
    pallas_call x1, Pallas kernels, on_device(): pl.pallas_call(functools.partial(kernel, (grp_size, pos_size, S, TR, M)),...  61 us
    unnamed x2, local copies, waits for them, and re-layouts  1.77 us

profile of v3, /device:TPU:0, one launch (start us, length us, event | category | flops | bytes accessed | tf_op | source)
XLA Modules:
  0.0 63.4 jit_solution(11754039156457071260)
XLA Ops:
  0.6 61.0 %shard_map.77 = (f32[2,1024,128]{2,1,0:T(8,128)S(1)}, f32[2,256,256]{2,1,0:T(8,128)S(1)}) custom-call(s32[2,3]{1,0:T(2,128)} %corners.1, s32[32]{0:T(128)} %counts.1, f32[2,1024,128]{2,1,0:T(8,128)} %obj_hbm.1, f32[2,256,256]{2,1,0:T(8,128)} %prb_hbm.1, f32[3,256,256]{2,1,0:T(8,128)} %pat_hbm.1, bf16[2,2,512,512]{3,2,1,0:T(8,128)(2,1)} %constant.2.clone.tab_hbm), custom_call_target="tpu_custom_call" | custom-call | tf_op jit(solution)/shard_map/pallas_call | solution.py:406
  61.7 1.0 %copy.10 = f32[2,1024,128]{2,1,0:T(8,128)} copy(f32[2,1024,128]{2,1,0:T(8,128)S(1)} %get-tuple-element.2) | data formatting | bytes 2097152
  62.6 0.8 %copy.11 = f32[2,256,256]{2,1,0:T(8,128)} copy(f32[2,256,256]{2,1,0:T(8,128)S(1)} %get-tuple-element.3) | data formatting | bytes 1048576
